TPU v7x, 512 devices: a whole 4x4x16 slice. The times are simulated.
512 devices in a mesh: expert: 64 (over z, y), replica: 8 (over x, core).
Axes of the slice: x: 4, y: 4, z: 16, core: 2. Of those that a mesh axis runs over, the one named last changes fastest.
Arguments:
- cotangent: bfloat16 [65536, 2048], P(('expert', 'replica')), may hold values from -2 to 2
- hidden: bfloat16 [65536, 6, 704], P(('expert', 'replica')), may hold values from -24 to 24
- routes: int32 [65536, 6], P(('expert', 'replica')), may hold values from 0 to 63, all different within a row; in each aligned block of 128 rows (0 to 127, 128 to 255, ...) at most 18 rows name the same one
- numerators: int32 [65536, 6], P(('expert', 'replica')), may hold values from 1 to 1024
- w_down: bfloat16 [64, 704, 2048], P('expert'), may hold values from -0.21875 to 0.21875
Outputs:
- gate_grad: float32 [65536, 6], P(('expert', 'replica'))
- grad_scales: float32 [64, 704, 16], P('expert', 'replica')
- grad_mantissa: float32 [64, 704, 2048], P('expert', 'replica')
Inputs may be any that keep to these rules, and one draw needn't show every extreme that they name: `routes`: no expert is named by more than 18 rows of one device's tokens, a bound that some blocks reach.
All inputs are finite; a program needn't handle non-finite values. Where the computation divides by a largest or mean magnitude, that divisor is 1e-20 or more.
Results may differ from a plain program's by a relative error of at most 0.023.
Values may be sent and summed in bfloat16 or wider, within the bound.
A program may use at most 64 MiB of HBM per device.

v0:
```python
import jax
import jax.numpy as jnp
from jax import lax
from jax.sharding import PartitionSpec as P

BLOCK = 128


def per_device(cotangent, hidden, routes, numerators, w_down):
    tok_count = cotangent.shape[0]
    model_width = cotangent.shape[1]
    top_k = hidden.shape[1]
    hidden_width = hidden.shape[2]
    experts = lax.axis_size("expert")
    replicas = lax.axis_size("replica")
    slot_count = 3 * tok_count * top_k // (2 * experts)
    routed = tok_count * top_k
    total_slots = experts * slot_count
    flat_routes = routes.reshape(routed)
    one_hot = (flat_routes[:, None] == jnp.arange(experts, dtype=jnp.int32)[None, :]).astype(
        jnp.int32
    )
    before = jnp.cumsum(one_hot, axis=0) - one_hot
    rank_in = jnp.sum(before * one_hot, axis=1)
    slot_of = flat_routes * slot_count + rank_in
    source_row = (
        jnp.full((total_slots,), routed, jnp.int32)
        .at[slot_of]
        .set(jnp.arange(routed, dtype=jnp.int32))
    )
    in_use = source_row < routed
    token_row = jnp.where(in_use, source_row // top_k, tok_count)
    padded_cot = jnp.concatenate([cotangent, jnp.zeros((1, model_width), cotangent.dtype)], axis=0)
    send_cot = padded_cot[token_row].reshape(experts, slot_count, model_width)
    padded_hid = jnp.concatenate(
        [hidden.reshape(routed, hidden_width), jnp.zeros((1, hidden_width), hidden.dtype)], axis=0
    )
    send_hid = padded_hid[source_row].reshape(experts, slot_count, hidden_width)
    weights_flat = numerators.reshape(routed).astype(jnp.float32) / 1024.0
    padded_w = jnp.concatenate([weights_flat, jnp.zeros((1,), jnp.float32)], axis=0)
    send_w = padded_w[source_row].reshape(experts, slot_count)
    matrix = w_down[0]
    contract_width = (((1,), (1,)), ((), ()))
    got_cot, got_w, got_hid = (
        lax.all_to_all(send_cot, "expert", split_axis=0, concat_axis=0, tiled=True),
        lax.all_to_all(
            send_w.astype(jnp.bfloat16), "expert", split_axis=0, concat_axis=0, tiled=True
        ).astype(send_w.dtype),
        lax.all_to_all(send_hid, "expert", split_axis=0, concat_axis=0, tiled=True),
    )
    cot_flat = got_cot.reshape(total_slots, model_width)
    back_proj = lax.dot_general(
        cot_flat, matrix, contract_width, preferred_element_type=jnp.float32
    )
    hid_flat = got_hid.reshape(total_slots, hidden_width)
    gate_local = jnp.sum(back_proj * hid_flat.astype(jnp.float32), axis=1)
    returned = lax.all_to_all(
        gate_local.reshape(experts, slot_count), "expert", split_axis=0, concat_axis=0, tiled=True
    )
    gate_grad = returned.reshape(total_slots)[slot_of].reshape(tok_count, top_k)
    scaled = (got_w.reshape(total_slots)[:, None] * cot_flat.astype(jnp.float32)).astype(
        jnp.bfloat16
    )
    partial_value = lax.dot_general(
        hid_flat, scaled, (((0,), (0,)), ((), ())), preferred_element_type=jnp.float32
    )
    blocks = partial_value.reshape(hidden_width, model_width // BLOCK, BLOCK)
    local_max = jnp.max(jnp.abs(blocks), axis=2)
    scales = lax.pmax(local_max.astype(jnp.bfloat16), "replica").astype(local_max.dtype) + 1e-06
    mantissa = (blocks / scales[:, :, None]).astype(jnp.bfloat16)
    mantissa = (
        lax.optimization_barrier(mantissa).astype(jnp.float32).reshape(hidden_width, model_width)
    )
    share_rows = hidden_width // replicas
    share_start = lax.axis_index("replica") * share_rows
    whole_sum = lax.psum(mantissa.astype(jnp.bfloat16), "replica").astype(jnp.float32)
    summed = lax.dynamic_slice_in_dim(whole_sum, share_start, share_rows, 0)
    scale_share = lax.dynamic_slice_in_dim(scales, share_start, share_rows, 0)
    return (gate_grad, scale_share[None], summed[None])


def solution(mesh):
    return jax.shard_map(
        per_device,
        mesh=mesh,
        in_specs=(
            P(("expert", "replica"), None),
            P(("expert", "replica"), None, None),
            P(("expert", "replica"), None),
            P(("expert", "replica"), None),
            P("expert", None, None),
        ),
        out_specs=(
            P(("expert", "replica"), None),
            P("expert", "replica", None),
            P("expert", "replica", None),
        ),
        check_vma=False,
    )
```

profile of v0, /device:TPU:1, one launch (start us, length us, event | category | flops | bytes accessed | tf_op | source)
XLA Modules:
  0.0 614.9 jit_solution(7978967521401818478)
XLA Ops:
  7.2 0.8 broadcast_multiply_fusion
  9.4 1.8 reduce-window.6
  11.7 3.4 scatter_custom_fusion
  16.1 7.3 %gather_fusion.3 = bf16[1152]{0:T(1024)(128)(2,1)S(1)} fusion(bf16[769]{0:T(1024)(128)(2,1)S(1)} %pad_maximum_fusion, s32[2048]{0:T(1024)S(1)} %get-tuple-element.13), kind=kCustom, calls=%fused_computation.3 | custom fusion | bytes 9216 | tf_op jit(solution)/shard_map/gather | solution.py:41
  24.2 19.3 %all-to-all-start.3 = ((bf16[64,1,18]{2,1,0:T(2,128)(2,1)}), bf16[64,1,18]{2,1,0:T(2,128)(2,1)S(1)}, u32[]{:S(2)}, u32[]{:S(2)}) async-start(bf16[64,1,18]{2,1,0:T(2,128)(2,1)} %convert_element_type.76), calls=%async_computation.3 | async-start | bytes 65536 | tf_op jit(solution)/shard_map/all_to_all | solution.py:46
  43.5 2.9 copy.26
  46.4 3.3 reshape.111
  49.7 2.4 concatenate.10
  52.1 7.1 %gather_fusion.1 = bf16[1152,704]{1,0:T(8,128)(2,1)} fusion(bf16[769,704]{1,0:T(8,128)(2,1)} %concatenate.10, s32[2048]{0:T(1024)S(1)} %get-tuple-element.13), kind=kCustom, calls=%fused_computation.1 | custom fusion | bytes 3248640 | tf_op jit(solution)/shard_map/gather | solution.py:38
  59.2 4.1 reshape.112
  63.3 14.8 %all-to-all-start.1 = ((bf16[64,18,704]{2,1,0:T(8,128)(2,1)}), bf16[64,18,704]{2,1,0:T(8,128)(2,1)}, u32[]{:S(2)}, u32[]{:S(2)}) async-start(bf16[64,18,704]{2,1,0:T(8,128)(2,1)} %reshape.112), calls=%async_computation.1 | async-start | bytes 4718592 | tf_op jit(solution)/shard_map/all_to_all | solution.py:49
  78.1 1.1 concatenate.9
  79.2 6.0 gather_fusion
  85.2 7.5 %reshape.109 = bf16[64,18,2048]{2,1,0:T(8,128)(2,1)} reshape(bf16[1152,2048]{1,0:T(8,128)(2,1)} %gather_fusion) | data formatting | bytes 9437184 | tf_op jit(solution)/shard_map/reshape | solution.py:34
  92.7 90.7 %all-to-all-done.1 = bf16[64,18,704]{2,1,0:T(8,128)(2,1)} async-done(((bf16[64,18,704]{2,1,0:T(8,128)(2,1)}), bf16[64,18,704]{2,1,0:T(8,128)(2,1)}, u32[]{:S(2)}, u32[]{:S(2)}) %all-to-all-start.1) | async-done | bytes 1622048 | tf_op jit(solution)/shard_map/all_to_all | solution.py:49
  183.4 11.1 %all-to-all-start = ((bf16[64,18,2048]{2,1,0:T(8,128)(2,1)}), bf16[64,18,2048]{2,1,0:T(8,128)(2,1)}, u32[]{:S(2)}, u32[]{:S(2)}) async-start(bf16[64,18,2048]{2,1,0:T(8,128)(2,1)} %reshape.109), calls=%async_computation | async-start | bytes 12582912 | tf_op jit(solution)/shard_map/all_to_all | solution.py:45
  195.0 4.1 reshape.113
  199.2 268.0 %all-to-all-done = bf16[64,18,2048]{2,1,0:T(8,128)(2,1)} async-done(((bf16[64,18,2048]{2,1,0:T(8,128)(2,1)}), bf16[64,18,2048]{2,1,0:T(8,128)(2,1)}, u32[]{:S(2)}, u32[]{:S(2)}) %all-to-all-start) | async-done | bytes 4718624 | tf_op jit(solution)/shard_map/all_to_all | solution.py:45
  467.1 7.7 %reshape.110 = bf16[1152,2048]{1,0:T(8,128)(2,1)} reshape(bf16[64,18,2048]{2,1,0:T(8,128)(2,1)} %all-to-all-done) | data formatting | bytes 9437184 | tf_op jit(solution)/shard_map/reshape | solution.py:51
  474.8 5.4 fusion
  480.1 6.8 %copy.37 = bf16[2048,1152]{1,0:T(8,128)(2,1)} copy(bf16[2048,1152]{0,1:T(8,128)(2,1)} %fusion) | data formatting | bytes 9437184 | tf_op jit(solution)/shard_map/dot_general | solution.py:64
  486.9 9.0 %abs_reduce_fusion = (bf16[704,16]{0,1:T(8,128)(2,1)S(1)}, f32[704,16,128]{2,0,1:T(8,128)}) fusion(bf16[16,128,1152]{2,1,0:T(8,128)(2,1)} %bitcast.45, bf16[1152,704]{1,0:T(8,128)(2,1)} %reshape.113), kind=kOutput, calls=%fused_computation.7 | convolution fusion | flops 3326202880 | bytes 12130304 | tf_op jit(solution)/shard_map/dot_general | solution.py:64
  496.0 28.4 %pmax.7 = bf16[704,16]{0,1:T(8,128)(2,1)S(1)} all-reduce(bf16[704,16]{0,1:T(8,128)(2,1)S(1)} %get-tuple-element.11), channel_id=1, replica_groups=mesh['expert'=64,'replica'=8] {'replica'}, use_global_device_ids=true, to_apply=%region_6.7 | all-reduce | flops 11264 | bytes 45056 | tf_op jit(solution)/shard_map/pmax | solution.py:69
  524.3 4.3 divide_convert_fusion
  528.6 2.0 copy_bitcast_fusion
  530.6 3.8 copy.27
  534.4 6.8 %fusion.4 = f32[1152]{0:T(1024)S(1)} fusion(bf16[1152,704]{0,1:T(8,128)(2,1)} %copy.27, bf16[1152,2048]{1,0:T(8,128)(2,1)} %reshape.110, bf16[1,704,2048]{2,1,0:T(8,128)(2,1)S(1)} %copy-done), kind=kOutput, calls=%fused_computation.14 | convolution fusion | flops 3324320768 | bytes 9228800 | tf_op jit(solution)/shard_map/dot_general | solution.py:52
  542.0 6.9 %all-to-all-start.2 = ((f32[64,1,18]{2,1,0:T(1,128)}), f32[64,1,18]{2,1,0:T(1,128)S(1)}, u32[]{:S(2)}, u32[]{:S(2)}) async-start(f32[64,1,18]{2,1,0:T(1,128)} %bitcast.2), calls=%async_computation.2 | async-start | bytes 65536 | tf_op jit(solution)/shard_map/all_to_all | solution.py:57
  549.6 12.7 %all-to-all-done.2 = f32[64,1,18]{2,1,0:T(1,128)S(1)} async-done(((f32[64,1,18]{2,1,0:T(1,128)}), f32[64,1,18]{2,1,0:T(1,128)S(1)}, u32[]{:S(2)}, u32[]{:S(2)}) %all-to-all-start.2) | async-done | bytes 4640 | tf_op jit(solution)/shard_map/all_to_all | solution.py:57
  563.6 4.5 gather_fusion.2
  568.9 37.2 %all-reduce.4.cloned.1.call-done = bf16[704,2048]{1,0:T(8,128)(2,1)} async-done(((bf16[704,2048]{1,0:T(8,128)(2,1)}), bf16[704,2048]{1,0:T(8,128)(2,1)}) %all-reduce.4.cloned.1.call-update) | async-done | bytes 2883600 | tf_op jit(solution)/shard_map/psum | solution.py:76
  606.1 1.9 convert_bitcast_fusion
  (34 shorter events, 7.7 us)
Async XLA Ops:
  7.2 527.3 %copy-start = (bf16[1,704,2048]{2,1,0:T(8,128)(2,1)S(1)}, bf16[1,704,2048]{2,1,0:T(8,128)(2,1)}, u32[]{:S(2)}) copy-start(bf16[1,704,2048]{2,1,0:T(8,128)(2,1)} %param.9) | copy-start | bytes 8650756
  24.2 39.1 %all-to-all-start.3 = ((bf16[64,1,18]{2,1,0:T(2,128)(2,1)}), bf16[64,1,18]{2,1,0:T(2,128)(2,1)S(1)}, u32[]{:S(2)}, u32[]{:S(2)}) async-start(bf16[64,1,18]{2,1,0:T(2,128)(2,1)} %convert_element_type.76), calls=%async_computation.3 | async-start | bytes 65536 | tf_op jit(solution)/shard_map/all_to_all | solution.py:46
  63.3 120.1 %all-to-all-start.1 = ((bf16[64,18,704]{2,1,0:T(8,128)(2,1)}), bf16[64,18,704]{2,1,0:T(8,128)(2,1)}, u32[]{:S(2)}, u32[]{:S(2)}) async-start(bf16[64,18,704]{2,1,0:T(8,128)(2,1)} %reshape.112), calls=%async_computation.1 | async-start | bytes 4718592 | tf_op jit(solution)/shard_map/all_to_all | solution.py:49
  183.4 283.7 %all-to-all-start = ((bf16[64,18,2048]{2,1,0:T(8,128)(2,1)}), bf16[64,18,2048]{2,1,0:T(8,128)(2,1)}, u32[]{:S(2)}, u32[]{:S(2)}) async-start(bf16[64,18,2048]{2,1,0:T(8,128)(2,1)} %reshape.109), calls=%async_computation | async-start | bytes 12582912 | tf_op jit(solution)/shard_map/all_to_all | solution.py:45
  194.5 411.6 %all-reduce.4.cloned.1.call-start = ((), (), s32[]{:S(2)}) async-start(), calls=%async_computation.4 | async-start | bytes 5767168 | tf_op jit(solution)/shard_map/psum | solution.py:76
  542.0 20.3 %all-to-all-start.2 = ((f32[64,1,18]{2,1,0:T(1,128)}), f32[64,1,18]{2,1,0:T(1,128)S(1)}, u32[]{:S(2)}, u32[]{:S(2)}) async-start(f32[64,1,18]{2,1,0:T(1,128)} %bitcast.2), calls=%async_computation.2 | async-start | bytes 65536 | tf_op jit(solution)/shard_map/all_to_all | solution.py:57
Sparse Core Ops, SparseCore 0:
  530.7 75.3 all-reduce.3
where the time goes:
time: 617 us; the launch traced here: 615 us
  waiting for transfers between devices  409 us (66%)
  local copies, waits for them, and re-layouts  79.6 us (13%)
  starting transfers between devices  52.3 us (8%)
  blocking collectives  28.4 us (5%)
  other arithmetic  15.9 us (3%)
  matrix products  15.8 us (3%)
  between operations  14.2 us (2%)
    all_to_all x1, waiting for transfers between devices, per_device(): lax.all_to_all(send_cot, 'expert', split_axis=0, concat_axis=0, tiled=True)  268 us
    all_to_all x1, waiting for transfers between devices, per_device(): lax.all_to_all(send_hid, 'expert', split_axis=0, concat_axis=0, tiled=True)  90.7 us
    psum x1, waiting for transfers between devices, per_device(): lax.psum(mantissa.astype(jnp.bfloat16), 'replica').astype(jnp.float32)  37.2 us
    pmax x1, blocking collectives, per_device(): lax.pmax(local_max.astype(jnp.bfloat16), 'replica').astype(local_max.dtype)  28.4 us
    all_to_all x1, starting transfers between devices, per_device(): lax.all_to_all(send_w.astype(jnp.bfloat16), 'expert', split_axis=0, conca...  19.3 us
    all_to_all x1, starting transfers between devices, per_device(): lax.all_to_all(send_hid, 'expert', split_axis=0, concat_axis=0, tiled=True)  14.8 us
    all_to_all x1, waiting for transfers between devices, per_device(): lax.all_to_all(gate_local.reshape(experts, slot_count), 'expert', split_a...  12.7 us
  transfers between devices with their start and end apart: 5, of which 4 were waited for; matrix products, arithmetic and copies ran while one was open for 9% of the time, Pallas kernels for 0%

commit v1 on v0

v1 whole, which is shorter than its diff:
```python
import jax
import jax.numpy as jnp
from jax import lax
from jax.sharding import Mesh, PartitionSpec as P

BLOCK = 128
NZ, NY, NX, NC = 16, 4, 4, 2
SLOTS = 18
COLS = 768


def per_device(cotangent, hidden, routes, numerators, w_down):
    tok, width = cotangent.shape
    top, hid = hidden.shape[1], hidden.shape[2]
    routed = tok * top
    experts = NZ * NY
    flat = routes.reshape(routed)
    one_hot = flat[:, None] == jnp.arange(experts, dtype=jnp.int32)[None, :]
    one_hot_b = one_hot.astype(jnp.bfloat16)
    row = jnp.arange(routed, dtype=jnp.int32)
    lower = (row[:, None] > row[None, :]).astype(jnp.bfloat16)
    before = jnp.dot(lower, one_hot_b, preferred_element_type=jnp.float32)
    rank = jnp.sum(jnp.where(one_hot, before, 0.0), axis=1).astype(jnp.int32)
    slot = flat * SLOTS + rank
    pack = (jnp.arange(experts * SLOTS, dtype=jnp.int32)[:, None] == slot[None, :]).astype(
        jnp.bfloat16
    )
    flat_n = numerators.reshape(routed)
    extra = jnp.concatenate(
        [
            (flat_n // 32).astype(jnp.bfloat16)[:, None],
            (flat_n % 32).astype(jnp.bfloat16)[:, None],
            jnp.zeros((routed, COLS - hid - 2), jnp.bfloat16),
        ],
        axis=1,
    )
    rows = jnp.concatenate([hidden.reshape(routed, hid), extra], axis=1)
    packed = jnp.dot(pack, rows, preferred_element_type=jnp.float32).astype(jnp.bfloat16)
    held = jnp.max(
        jnp.where(one_hot, rank[:, None] + 1, 0).reshape(tok, top, experts), axis=1
    )
    table = (held - 1).T.astype(jnp.float32).reshape(NZ, NY, tok)

    cots = lax.all_gather(cotangent, "z")
    ranks = lax.all_to_all(table, "z", split_axis=0, concat_axis=0, tiled=True)
    hid_z = lax.all_to_all(
        packed.reshape(NZ, NY * SLOTS, COLS), "z", split_axis=0, concat_axis=0, tiled=True
    )
    hid_y = hid_z.reshape(NZ, NY, SLOTS, COLS).transpose(1, 0, 2, 3)
    got_hid = lax.all_to_all(
        hid_y.reshape(NY, NZ * SLOTS, COLS), "y", split_axis=0, concat_axis=0, tiled=True
    ).reshape(experts * SLOTS, COLS)
    select = (
        ranks[:, :, None, :] == jnp.arange(SLOTS, dtype=jnp.float32)[None, None, :, None]
    ).astype(jnp.bfloat16)
    picked = lax.dot_general(
        select.reshape(NZ, NY * SLOTS, tok),
        cots,
        (((2,), (1,)), ((0,), (0,))),
        preferred_element_type=jnp.float32,
    ).astype(jnp.bfloat16)
    cot_y = picked.reshape(NZ, NY, SLOTS, width).transpose(1, 0, 2, 3)
    cot_rows = lax.all_to_all(
        cot_y.reshape(NY, NZ * SLOTS, width), "y", split_axis=0, concat_axis=0, tiled=True
    ).reshape(experts * SLOTS, width)

    hid_rows = got_hid[:, :hid]
    weight = (
        got_hid[:, hid].astype(jnp.float32) * 32.0 + got_hid[:, hid + 1].astype(jnp.float32)
    ) / 1024.0
    back = lax.dot_general(
        cot_rows, w_down[0], (((1,), (1,)), ((), ())), preferred_element_type=jnp.float32
    )
    gate = jnp.sum(back * hid_rows.astype(jnp.float32), axis=1)
    gate_y = lax.all_to_all(
        gate.reshape(NY, NZ * SLOTS), "y", split_axis=0, concat_axis=0, tiled=True
    )
    gate_z = lax.all_to_all(
        gate_y.reshape(NY, NZ, SLOTS).transpose(1, 0, 2).reshape(NZ, NY * SLOTS),
        "z",
        split_axis=0,
        concat_axis=0,
        tiled=True,
    )
    gate_grad = jnp.sum(
        jnp.where(pack > 0, gate_z.reshape(experts * SLOTS)[:, None], 0.0), axis=0
    ).reshape(tok, top)

    weighted = (hid_rows.astype(jnp.float32) * weight[:, None]).astype(jnp.bfloat16)
    partial_value = lax.dot_general(
        weighted, cot_rows, (((0,), (0,)), ((), ())), preferred_element_type=jnp.float32
    ).astype(jnp.bfloat16)
    replicas = NX * NC
    share = hid // replicas
    parts = lax.all_to_all(
        partial_value.reshape(replicas, share, width),
        ("x", "c"),
        split_axis=0,
        concat_axis=0,
        tiled=True,
    ).astype(jnp.float32)
    blocks = parts.reshape(replicas, share, width // BLOCK, BLOCK)
    scales = jnp.max(jnp.max(jnp.abs(blocks), axis=3), axis=0) + 1e-6
    total = jnp.sum(blocks, axis=0) / scales[:, :, None]
    return gate_grad, scales[None], total.reshape(1, share, width)


def solution(mesh):
    fine = Mesh(mesh.devices.reshape(NZ, NY, NX, NC), ("z", "y", "x", "c"))
    every = ("z", "y", "x", "c")
    expert, replica = ("z", "y"), ("x", "c")
    return jax.shard_map(
        per_device,
        mesh=fine,
        in_specs=(
            P(every, None),
            P(every, None, None),
            P(every, None),
            P(every, None),
            P(expert, None, None),
        ),
        out_specs=(
            P(every, None),
            P(expert, replica, None),
            P(expert, replica, None),
        ),
        check_vma=False,
    )
```

time: 617 us -> 372 us (0.60)
  waiting for transfers between devices: 409 us -> 230 us
  local copies, waits for them, and re-layouts: 79.6 us -> 37.4 us
  blocking collectives: 28.4 us -> 0 us
  matrix products: 15.8 us -> 24.6 us
  other arithmetic: 15.9 us -> 9.64 us
    all_to_all x4 -> x7, waiting for transfers between devices: 371 us -> 192 us  [the longest x1 98 us: per_device(): lax.all_to_all(packed.reshape(NZ, NY * SLOTS, COLS), 'z', split_axis=0, c...]
    psum x1 -> x0, waiting for transfers between devices: 37.2 us -> none  [per_device(): lax.psum(mantissa.astype(jnp.bfloat16), 'replica').astype(jnp.float32)]
    all_gather x0 -> x1, waiting for transfers between devices: none -> 37 us  [per_device(): cots = lax.all_gather(cotangent, 'z')]
    pmax x1 -> x0, blocking collectives: 28.4 us -> none  [per_device(): lax.pmax(local_max.astype(jnp.bfloat16), 'replica').astype(local_max.dtype)]
    gather x4 -> x0, local copies, waits for them, and re-layouts: 24.9 us -> none  [the longest x1 7.27 us: per_device(): send_w = padded_w[source_row].reshape(experts, slot_count)]
    reshape x8 -> x7, local copies, waits for them, and re-layouts: 30.8 us -> 10 us  [the longest x1 4.75 us: per_device(): cot_y.reshape(NY, NZ * SLOTS, width)]
    dot_general x2 -> x5, matrix products: 15.8 us -> 24.6 us  [the longest x1 8.33 us: per_device(): lax.dot_general(weighted, cot_rows, (((0,), (0,)), ((), ())), preferred_e...]
    dot_general x1 -> x0, local copies, waits for them, and re-layouts: 6.79 us -> none  [per_device(): lax.dot_general(hid_flat, scaled, (((0,), (0,)), ((), ())), preferred_ele...]
  transfers between devices with their start and end apart: 5 -> 8, of which waited for: 4 -> 7; matrix products, arithmetic and copies ran while one was open for 9% -> 14% of each run, Pallas kernels for 0% -> 0%
where the time goes in v1:
time: 372 us; the launch traced here: 371 us
  waiting for transfers between devices  230 us (62%)
  starting transfers between devices  54.8 us (15%)
  local copies, waits for them, and re-layouts  37.4 us (10%)
  matrix products  24.6 us (7%)
  between operations  14.3 us (4%)
  other arithmetic  9.64 us (3%)
    all_to_all x1, waiting for transfers between devices, per_device(): lax.all_to_all(packed.reshape(NZ, NY * SLOTS, COLS), 'z', split_axis=0, c...  98 us
    all_to_all x1, waiting for transfers between devices, per_device(): lax.all_to_all(cot_y.reshape(NY, NZ * SLOTS, width), 'y', split_axis=0, c...  48.1 us
    all_gather x1, waiting for transfers between devices, per_device(): cots = lax.all_gather(cotangent, 'z')  37 us
    all_to_all x1, waiting for transfers between devices, per_device(): lax.all_to_all(partial_value.reshape(replicas, share, width), ('x', 'c'),...  32.2 us
    all_to_all x1, starting transfers between devices, per_device(): lax.all_to_all(packed.reshape(NZ, NY * SLOTS, COLS), 'z', split_axis=0, c...  15.9 us
    unnamed x13, local copies, waits for them, and re-layouts  11.1 us
    all_to_all x1, starting transfers between devices, per_device(): ranks = lax.all_to_all(table, 'z', split_axis=0, concat_axis=0, tiled=True)  8.9 us
    all_to_all x1, starting transfers between devices, per_device(): lax.all_to_all(gate_y.reshape(NY, NZ, SLOTS).transpose(1, 0, 2).reshape(N...  8.6 us
  transfers between devices with their start and end apart: 8, of which 7 were waited for; matrix products, arithmetic and copies ran while one was open for 14% of the time, Pallas kernels for 0%

profile of v1, /device:TPU:1, one launch (start us, length us, event | category | flops | bytes accessed | tf_op | source)
XLA Modules:
  0.0 370.8 jit_solution(15814460167081239903)
XLA Ops:
  9.9 2.9 copy.97
  12.8 3.3 reshape.242
  17.0 4.4 %fusion.3 = bf16[1152,768]{1,0:T(8,128)(2,1)} fusion(s32[768]{0:T(1024)S(1)} %get-tuple-element.27, bf16[768,1]{1,0:T(8,128)(2,1)S(1)} %get-tuple-element.23, bf16[768,1]{1,0:T(8,128)(2,1)S(1)} %get-tuple-element.22, bf16[768,704]{1,0:T(8,128)(2,1)} %reshape.242, bf16[768]{0:T(1024)(128)(2,1)S(1)} %pad.3.clone), kind=kOutput, calls=%fused_computation.10 | convolution fusion | flops 1365442560 | bytes 2858496 | tf_op jit(solution)/shard_map/dot_general | solution.py:38
  21.4 15.9 %all-to-all-start.2 = ((bf16[16,72,768]{2,1,0:T(8,128)(2,1)}), bf16[16,72,768]{2,1,0:T(8,128)(2,1)}, u32[]{:S(2)}, u32[]{:S(2)}) async-start(bf16[16,72,768]{2,1,0:T(8,128)(2,1)} %bitcast.43), calls=%async_computation.2 | async-start | bytes 3538944 | tf_op jit(solution)/shard_map/all_to_all | solution.py:46
  38.2 98.0 %all-to-all-done.2 = bf16[16,72,768]{2,1,0:T(8,128)(2,1)} async-done(((bf16[16,72,768]{2,1,0:T(8,128)(2,1)}), bf16[16,72,768]{2,1,0:T(8,128)(2,1)}, u32[]{:S(2)}, u32[]{:S(2)}) %all-to-all-start.2) | async-done | bytes 1769504 | tf_op jit(solution)/shard_map/all_to_all | solution.py:46
  136.2 8.9 %all-to-all-start = ((f32[16,4,128]{2,1,0:T(4,128)}), f32[16,4,128]{2,1,0:T(4,128)S(1)}, u32[]{:S(2)}, u32[]{:S(2)}) async-start(f32[16,4,128]{2,1,0:T(4,128)} %bitcast.1), calls=%async_computation | async-start | bytes 65536 | tf_op jit(solution)/shard_map/all_to_all | solution.py:45
  145.1 1.8 copy.103
  147.0 1.4 copy.104
  148.3 1.5 copy.105
  149.8 7.0 %all-to-all-done = f32[16,4,128]{2,1,0:T(4,128)S(1)} async-done(((f32[16,4,128]{2,1,0:T(4,128)}), f32[16,4,128]{2,1,0:T(4,128)S(1)}, u32[]{:S(2)}, u32[]{:S(2)}) %all-to-all-start) | async-done | bytes 32800 | tf_op jit(solution)/shard_map/all_to_all | solution.py:45
  156.8 4.6 %all-to-all-start.3 = ((bf16[4,288,768]{2,1,0:T(8,128)(2,1)}), bf16[4,288,768]{2,1,0:T(8,128)(2,1)}, u32[]{:S(2)}, u32[]{:S(2)}) async-start(bf16[4,288,768]{2,1,0:T(8,128)(2,1)} %copy.105), calls=%async_computation.3 | async-start | bytes 3538944 | tf_op jit(solution)/shard_map/all_to_all | solution.py:50
  161.6 37.0 %all-gather.3.cloned.1.call-done = bf16[2048,2048]{1,0:T(8,128)(2,1)} async-done(((bf16[128,2048]{1,0:T(8,128)(2,1)}), bf16[2048,2048]{1,0:T(8,128)(2,1)}) %all-gather.3.cloned.1.call-update) | async-done | bytes 8388624 | tf_op jit(solution)/shard_map/all_gather | solution.py:44
  198.6 4.8 %convolution_convert_fusion = bf16[16,72,2048]{2,1,0:T(8,128)(2,1)S(1)} fusion(bf16[16,128,2048]{2,1,0:T(8,128)(2,1)} %bitcast.35, pred[16,72,128]{2,0,1:T(8,128)(4,1)S(1)} %bitcast_compare_fusion), kind=kOutput, calls=%fused_computation.5 | convolution fusion | flops 606339072 | bytes 13254656 | tf_op jit(solution)/shard_map/dot_general | solution.py:56
  203.4 2.6 copy.94
  206.0 3.6 copy.95
  209.6 4.8 %copy.96 = bf16[4,288,2048]{2,1,0:T(8,128)(2,1)} copy(bf16[4,288,2048]{2,0,1:T(4,128)(2,1)S(1)} %bitcast.37) | data formatting | bytes 9437184 | tf_op jit(solution)/shard_map/reshape | solution.py:64
  214.4 5.2 %all-to-all-start.1 = ((bf16[4,288,2048]{2,1,0:T(8,128)(2,1)}), bf16[4,288,2048]{2,1,0:T(8,128)(2,1)}, u32[]{:S(2)}, u32[]{:S(2)}) async-start(bf16[4,288,2048]{2,1,0:T(8,128)(2,1)} %copy.96), calls=%async_computation.1 | async-start | bytes 9437184 | tf_op jit(solution)/shard_map/all_to_all | solution.py:63
  219.5 1.4 fusion.30
  221.2 3.8 %copy.113 = bf16[1152,704]{0,1:T(8,128)(2,1)} copy(bf16[1152,704]{1,0:T(8,128)(2,1)} %bitcast.34) | data formatting | bytes 3244032
  225.1 48.1 %all-to-all-done.1 = bf16[4,288,2048]{2,1,0:T(8,128)(2,1)} async-done(((bf16[4,288,2048]{2,1,0:T(8,128)(2,1)}), bf16[4,288,2048]{2,1,0:T(8,128)(2,1)}, u32[]{:S(2)}, u32[]{:S(2)}) %all-to-all-start.1) | async-done | bytes 4718624 | tf_op jit(solution)/shard_map/all_to_all | solution.py:63
  273.2 6.8 %fusion.10 = f32[1152]{0:T(1024)S(1)} fusion(bf16[1152,704]{0,1:T(8,128)(2,1)} %copy.113, bf16[1152,2048]{1,0:T(8,128)(2,1)} %bitcast.7, bf16[1,704,2048]{2,1,0:T(8,128)(2,1)S(1)} %copy-done), kind=kOutput, calls=%fused_computation.18 | convolution fusion | flops 3324320768 | bytes 9228800 | tf_op jit(solution)/shard_map/dot_general | solution.py:71
  280.6 3.2 all-to-all-start.4
  283.9 4.1 %all-to-all-done.4 = f32[4,1,288]{2,1,0:T(1,128)S(1)} async-done(((f32[4,1,288]{2,1,0:T(1,128)}), f32[4,1,288]{2,1,0:T(1,128)S(1)}, u32[]{:S(2)}, u32[]{:S(2)}) %all-to-all-start.4) | async-done | bytes 4640 | tf_op jit(solution)/shard_map/all_to_all | solution.py:75
  288.9 8.6 %all-to-all-start.5 = ((f32[16,1,72]{2,1,0:T(1,128)}), f32[16,1,72]{2,1,0:T(1,128)S(1)}, u32[]{:S(2)}, u32[]{:S(2)}) async-start(f32[16,1,72]{2,1,0:T(1,128)} %bitcast.15), calls=%async_computation.5 | async-start | bytes 16384 | tf_op jit(solution)/shard_map/all_to_all | solution.py:78
  297.5 8.3 %convolution_convert_fusion.1 = bf16[704,2048]{1,0:T(8,128)(2,1)} fusion(bf16[1152,2048]{1,0:T(8,128)(2,1)} %bitcast.7, bf16[1152,704]{0,1:T(8,128)(2,1)} %copy.113, f32[1152]{0:T(1024)S(1)} %multiply_reduce_fusion), kind=kOutput, calls=%fused_computation.11 | convolution fusion | flops 3325763584 | bytes 9228800 | tf_op jit(solution)/shard_map/dot_general | solution.py:90
  305.8 2.9 all-to-all-done.5
  308.7 8.4 %all-to-all-start.6 = ((bf16[8,88,2048]{2,1,0:T(8,128)(2,1)}), bf16[8,88,2048]{2,1,0:T(8,128)(2,1)}, u32[]{:S(2)}, u32[]{:S(2)}) async-start(bf16[8,88,2048]{2,1,0:T(8,128)(2,1)} %bitcast.40), calls=%async_computation.6 | async-start | bytes 5767168 | tf_op jit(solution)/shard_map/all_to_all | solution.py:95
  319.8 32.2 %all-to-all-done.6 = bf16[8,88,2048]{2,1,0:T(8,128)(2,1)} async-done(((bf16[8,88,2048]{2,1,0:T(8,128)(2,1)}), bf16[8,88,2048]{2,1,0:T(8,128)(2,1)}, u32[]{:S(2)}, u32[]{:S(2)}) %all-to-all-start.6) | async-done | bytes 2883616 | tf_op jit(solution)/shard_map/all_to_all | solution.py:95
  352.0 3.4 convert_reduce_fusion
  356.4 1.4 reduce_max.32
  359.6 2.1 div.42
  361.7 2.3 bitcast_divide_fusion
  (42 shorter events, 12.0 us)
Async XLA Ops:
  7.2 266.0 %copy-start = (bf16[1,704,2048]{2,1,0:T(8,128)(2,1)S(1)}, bf16[1,704,2048]{2,1,0:T(8,128)(2,1)}, u32[]{:S(2)}) copy-start(bf16[1,704,2048]{2,1,0:T(8,128)(2,1)} %param.9) | copy-start | bytes 8650756
  7.2 191.4 %all-gather.3.cloned.1.call-start = ((), (), s32[]{:S(2)}) async-start(), calls=%async_computation.7 | async-start | bytes 8912896 | tf_op jit(solution)/shard_map/all_gather | solution.py:44
  21.4 16.1 %copy-start.1 = (s32[128,6]{0,1:T(8,128)S(1)}, s32[128,6]{0,1:T(8,128)}, u32[]{:S(2)}) copy-start(s32[128,6]{0,1:T(8,128)} %param.7) | copy-start | bytes 9220
  21.4 114.8 %all-to-all-start.2 = ((bf16[16,72,768]{2,1,0:T(8,128)(2,1)}), bf16[16,72,768]{2,1,0:T(8,128)(2,1)}, u32[]{:S(2)}, u32[]{:S(2)}) async-start(bf16[16,72,768]{2,1,0:T(8,128)(2,1)} %bitcast.43), calls=%async_computation.2 | async-start | bytes 3538944 | tf_op jit(solution)/shard_map/all_to_all | solution.py:46
  136.2 20.6 %all-to-all-start = ((f32[16,4,128]{2,1,0:T(4,128)}), f32[16,4,128]{2,1,0:T(4,128)S(1)}, u32[]{:S(2)}, u32[]{:S(2)}) async-start(f32[16,4,128]{2,1,0:T(4,128)} %bitcast.1), calls=%async_computation | async-start | bytes 65536 | tf_op jit(solution)/shard_map/all_to_all | solution.py:45
  156.8 57.6 %all-to-all-start.3 = ((bf16[4,288,768]{2,1,0:T(8,128)(2,1)}), bf16[4,288,768]{2,1,0:T(8,128)(2,1)}, u32[]{:S(2)}, u32[]{:S(2)}) async-start(bf16[4,288,768]{2,1,0:T(8,128)(2,1)} %copy.105), calls=%async_computation.3 | async-start | bytes 3538944 | tf_op jit(solution)/shard_map/all_to_all | solution.py:50
  214.4 58.8 %all-to-all-start.1 = ((bf16[4,288,2048]{2,1,0:T(8,128)(2,1)}), bf16[4,288,2048]{2,1,0:T(8,128)(2,1)}, u32[]{:S(2)}, u32[]{:S(2)}) async-start(bf16[4,288,2048]{2,1,0:T(8,128)(2,1)} %copy.96), calls=%async_computation.1 | async-start | bytes 9437184 | tf_op jit(solution)/shard_map/all_to_all | solution.py:63
  280.6 7.4 %all-to-all-start.4 = ((f32[4,1,288]{2,1,0:T(1,128)}), f32[4,1,288]{2,1,0:T(1,128)S(1)}, u32[]{:S(2)}, u32[]{:S(2)}) async-start(f32[4,1,288]{2,1,0:T(1,128)} %all_to_all.31), calls=%async_computation.4 | async-start | bytes 12288 | tf_op jit(solution)/shard_map/all_to_all | solution.py:75
  288.9 19.8 %all-to-all-start.5 = ((f32[16,1,72]{2,1,0:T(1,128)}), f32[16,1,72]{2,1,0:T(1,128)S(1)}, u32[]{:S(2)}, u32[]{:S(2)}) async-start(f32[16,1,72]{2,1,0:T(1,128)} %bitcast.15), calls=%async_computation.5 | async-start | bytes 16384 | tf_op jit(solution)/shard_map/all_to_all | solution.py:78
  308.7 43.3 %all-to-all-start.6 = ((bf16[8,88,2048]{2,1,0:T(8,128)(2,1)}), bf16[8,88,2048]{2,1,0:T(8,128)(2,1)}, u32[]{:S(2)}, u32[]{:S(2)}) async-start(bf16[8,88,2048]{2,1,0:T(8,128)(2,1)} %bitcast.40), calls=%async_computation.6 | async-start | bytes 5767168 | tf_op jit(solution)/shard_map/all_to_all | solution.py:95
Sparse Core Ops, SparseCore 0:
  10.1 188.4 all-gather.2

commit v2 on v0

v2 whole, which is shorter than its diff:
```python
import jax
import jax.numpy as jnp
from jax import lax
from jax.experimental import pallas as pl
from jax.experimental.pallas import tpu as pltpu
from jax.sharding import PartitionSpec as P

MESH = pl.DeviceIdType.MESH
BF, F32 = jnp.bfloat16, jnp.float32
BLOCK = 128
NZ, NY, NR = 16, 4, 8
EXPERTS = NZ * NY
SLOTS = 18
TOK, WIDTH, HID, TOP = 128, 2048, 704, 6
PADH = 768
ROUTED = TOK * TOP
COLUMN = NZ * SLOTS
SHARE = HID // NR
DC = 256
ND = WIDTH // DC
HALF = NZ // 2
GROUP = HALF * SLOTS
PLANE = NY * SLOTS


def iota(shape, dim):
    return lax.broadcasted_iota(jnp.int32, shape, dim).astype(F32)


def one_where(condition):
    return jnp.where(condition, 1.0, 0.0).astype(BF)


def kernel(
    cot, hid6, routes, nums, w,
    gate_o, scale_o, grad_o,
    G, PK, HZ, YH, HY, hidL, hT, WS, SEL, YS, R, XS, XR, gacc, RK, GS, GM, GO, GR, G2,
    cot_sem, hid_sem, w_sem, own_sem, ylocal, xlocal,
    ring_send, ring_recv, hz_sem, hy_sem, ys_send, ys_recv, xs_send, xs_recv, gy_sem, gz_sem,
):
    expert = lax.axis_index("expert")
    rep = lax.axis_index("replica")
    z = lax.div(expert, NY)
    y = lax.rem(expert, NY)

    def zat(d):
        return lax.rem(z + d, NZ)

    def zpeer(d):
        return (zat(d) * NY + y, rep)

    def ypeer(d):
        return (z * NY + lax.rem(y + d, NY), rep)

    def xpeer(d):
        return (expert, lax.rem(rep + d, NR))

    def remote(src, dst, send, recv, peer):
        return pltpu.make_async_remote_copy(
            src_ref=src, dst_ref=dst, send_sem=send, recv_sem=recv,
            device_id=peer, device_id_type=MESH,
        )

    cot_loads = [
        pltpu.make_async_copy(cot.at[:, pl.ds(j * DC, DC)], G.at[j, z], cot_sem.at[j])
        for j in range(ND)
    ]
    hid_loads = [
        pltpu.make_async_copy(
            hid6.at[k], hidL.at[pl.ds(0, HID), pl.ds(k * TOK, TOK)], hid_sem.at[k]
        )
        for k in range(TOP)
    ]
    w_loads = [
        pltpu.make_async_copy(
            w.at[:, pl.ds(j * DC, DC)], WS.at[j, pl.ds(0, HID), :], w_sem.at[j]
        )
        for j in range(ND)
    ]
    for copy in cot_loads + hid_loads + w_loads:
        copy.start()

    barrier = pltpu.get_barrier_semaphore()
    peers = (
        [zpeer(d) for d in range(1, NZ)]
        + [ypeer(d) for d in range(1, NY)]
        + [xpeer(d) for d in range(1, NR)]
    )
    for peer in peers:
        pl.semaphore_signal(barrier, inc=1, device_id=peer, device_id_type=MESH)
    pl.semaphore_wait(barrier, len(peers))

    steps = (HALF - 1, HALF)

    def ring_copy(way, j, s):
        slot = zat(NZ - s) if way == 0 else zat(s)
        peer = zpeer(1) if way == 0 else zpeer(NZ - 1)
        here = G.at[j, slot]
        return remote(here, here, ring_send.at[way, j], ring_recv.at[way, j, s], peer)

    def ring_arrival(way, j, s):
        slot = zat(NZ - 1 - s) if way == 0 else zat(1 + s)
        peer = zpeer(1) if way == 0 else zpeer(NZ - 1)
        here = G.at[j, slot]
        remote(here, here, ring_send.at[way, j], ring_recv.at[way, j, s], peer).wait_recv()

    for copy in cot_loads:
        copy.wait()
    for j in range(2):
        for way in range(2):
            ring_copy(way, j, 0).start()

    which = iota((EXPERTS, TOK), 0)
    names = [routes[k : k + 1, :].astype(F32) for k in range(TOP)]
    member = jnp.zeros((EXPERTS, TOK), F32)
    for k in range(TOP):
        member = member + jnp.where(which == names[k], 1.0, 0.0)
    earlier = one_where(iota((TOK, TOK), 0) < iota((TOK, TOK), 1))
    before = jnp.dot(member.astype(BF), earlier, preferred_element_type=F32)
    RK[...] = jnp.where(member > 0.5, before, -1.0)
    slot_row = jnp.concatenate(
        [
            names[k] * float(SLOTS)
            + jnp.sum(jnp.where(which == names[k], before, 0.0), axis=0, keepdims=True)
            for k in range(TOP)
        ],
        axis=1,
    )
    n_row = jnp.concatenate([nums[k : k + 1, :].astype(F32) for k in range(TOP)], axis=1)
    n_high = jnp.floor(n_row * (1.0 / 32.0))
    n_low = n_row - 32.0 * n_high
    t_row = jnp.concatenate([iota((1, TOK), 1) + 1.0] * TOP, axis=1)
    extra_row = iota((PADH - HID, ROUTED), 0)
    extra = jnp.where(
        extra_row == 0.0,
        n_high,
        jnp.where(extra_row == 1.0, n_low, jnp.where(extra_row == 2.0, t_row, 0.0)),
    )
    hidL[HID:PADH, :] = extra.astype(BF)
    WS[:, HID:PADH, :] = jnp.zeros((ND, PADH - HID, DC), BF)
    GO[...] = jnp.zeros_like(GO)
    gacc[...] = jnp.zeros_like(gacc)
    for copy in hid_loads:
        copy.wait()

    def pack(i, carry):
        rows = iota((NY * PLANE, 1), 0) + (i * (NY * PLANE)).astype(F32)
        chosen = one_where(rows == slot_row)
        out = lax.dot_general(
            chosen, hidL[...], (((1,), (1,)), ((), ())), preferred_element_type=F32
        )
        PK[pl.ds(i * NY, NY)] = out.reshape(NY, PLANE, PADH).astype(BF)
        return carry

    lax.fori_loop(0, NZ // NY, pack, 0)
    for d in (8, 7, 9, 6, 10, 5, 11, 4, 12, 3, 13, 2, 14, 1, 15):
        remote(PK.at[zat(d)], HZ.at[z], hz_sem.at[0], hz_sem.at[1], zpeer(d)).start()
    own_hz = pltpu.make_async_copy(PK.at[z], HZ.at[z], own_sem.at[0])
    own_hz.start()
    for copy in w_loads:
        copy.wait()

    def own_hy():
        return pltpu.make_async_copy(
            YH.at[y], HY.at[pl.ds(pl.multiple_of(y * COLUMN, COLUMN), COLUMN)], own_sem.at[1]
        )

    def hidden_mid():
        remote(
            HZ.at[pl.ds(0, NZ - 1)], HZ.at[pl.ds(0, NZ - 1)], hz_sem.at[0], hz_sem.at[1], zpeer(1)
        ).wait_recv()
        own_hz.wait()
        out_row = iota((NY * GROUP, 1), 0)
        out_y = jnp.floor((out_row + 0.5) * (1.0 / GROUP))
        rest = out_row - out_y * GROUP
        out_z = jnp.floor((rest + 0.5) * (1.0 / SLOTS))
        out_r = rest - out_z * SLOTS
        source = out_z * PLANE + out_y * SLOTS + out_r
        permute = one_where(iota((NY * GROUP, NY * GROUP), 1) == source)
        for g in range(2):
            block = HZ[g * HALF : (g + 1) * HALF].astype(F32)
            block = block.reshape(HALF * PLANE, PADH).astype(BF)
            out = jnp.dot(permute, block, preferred_element_type=F32)
            token = out[:, HID + 2 : HID + 3]
            target = jnp.where(token > 0.5, token + out_z * TOK - 1.0, -1.0)
            SEL[g] = one_where(iota((NY * GROUP, HALF * TOK), 1) == target)
            rows = out.astype(BF)
            for yy in range(NY):
                YH[yy, g * GROUP : (g + 1) * GROUP, :] = rows[yy * GROUP : (yy + 1) * GROUP]
        mine = HY.at[pl.ds(pl.multiple_of(y * COLUMN, COLUMN), COLUMN)]
        for d in range(1, NY):
            remote(YH.at[lax.rem(y + d, NY)], mine, hy_sem.at[0], hy_sem.at[1], ypeer(d)).start()
        own_hy().start()

    def hidden_end():
        three = HY.at[pl.ds(0, (NY - 1) * COLUMN)]
        remote(three, three, hy_sem.at[0], hy_sem.at[1], ypeer(1)).wait_recv()
        own_hy().wait()

        def turn(i, carry):
            start = pl.multiple_of(i * TOK, TOK)
            rows = HY[pl.ds(start, TOK), :].astype(F32)
            weight = (rows[:, HID : HID + 1] * 32.0 + rows[:, HID + 1 : HID + 2]) * (1.0 / 1024.0)
            hT[:, pl.ds(start, TOK)] = jnp.transpose(rows * weight).astype(BF)
            return carry

        lax.fori_loop(0, NY * COLUMN // TOK, turn, 0)

    def own_y(c):
        return pltpu.make_async_copy(YS.at[c, y], R.at[c, y], ylocal.at[c])

    def own_x(c):
        return pltpu.make_async_copy(XS.at[c, rep], XR.at[c, rep], xlocal.at[c])

    def select(c):
        for way in range(2):
            ring_arrival(way, c, steps[way] - 1)
        for g in range(2):
            block = G[c, g * HALF : (g + 1) * HALF].reshape(HALF * TOK, DC)
            out = jnp.dot(SEL[g], block, preferred_element_type=F32).astype(BF)
            for yy in range(NY):
                YS[c, yy, g * GROUP : (g + 1) * GROUP, :] = out[yy * GROUP : (yy + 1) * GROUP]
        for d in range(1, NY):
            remote(
                YS.at[c, lax.rem(y + d, NY)], R.at[c, y], ys_send.at[c], ys_recv.at[c], ypeer(d)
            ).start()
        own_y(c).start()

    def products(c):
        three = R.at[c, pl.ds(0, NY - 1)]
        remote(three, three, ys_send.at[c], ys_recv.at[c], ypeer(1)).wait_recv()
        own_y(c).wait()

        def part(i, carry):
            start = pl.multiple_of(i * (HID // 2), HID // 2)
            value = jnp.dot(
                hT[pl.ds(start, HID // 2), :],
                R[c].reshape(NY * COLUMN, DC),
                preferred_element_type=F32,
            )
            XS[c, pl.ds(i * (NR // 2), NR // 2)] = value.reshape(NR // 2, SHARE, DC).astype(BF)
            return carry

        lax.fori_loop(0, 2, part, 0)
        for d in range(1, NR):
            remote(
                XS.at[c, lax.rem(rep + d, NR)], XR.at[c, rep], xs_send.at[c], xs_recv.at[c], xpeer(d)
            ).start()
        own_x(c).start()

        def gates(b, carry):
            rows = HY[pl.ds(pl.multiple_of(b * COLUMN, COLUMN), COLUMN), :]
            value = jnp.dot(rows, WS[c], preferred_element_type=F32) * R[c, b].astype(F32)
            total = value[:, :BLOCK]
            for p in range(1, DC // BLOCK):
                total = total + value[:, p * BLOCK : (p + 1) * BLOCK]
            gacc[b] = gacc[b] + total
            return carry

        lax.fori_loop(0, NY, gates, 0)

    def finish(c):
        seven = XR.at[c, pl.ds(0, NR - 1)]
        remote(seven, seven, xs_send.at[c], xs_recv.at[c], xpeer(1)).wait_recv()
        own_x(c).wait()
        first = XR[c, 0].astype(F32)
        total, largest = first, jnp.abs(first)
        for q in range(1, NR):
            value = XR[c, q].astype(F32)
            total = total + value
            largest = jnp.maximum(largest, jnp.abs(value))
        lane = iota((SHARE, BLOCK), 1)
        for p in range(DC // BLOCK):
            cols = slice(p * BLOCK, (p + 1) * BLOCK)
            scale = jnp.max(largest[:, cols], axis=1, keepdims=True) + 1e-6
            start = pl.multiple_of(c * DC + p * BLOCK, BLOCK)
            grad_o[:, pl.ds(start, BLOCK)] = total[:, cols] / scale
            number = (c * (DC // BLOCK) + p).astype(F32)
            scale_o[...] = jnp.where(lane == number, scale, scale_o[...])

    scale_o[...] = jnp.zeros_like(scale_o)

    def own_gy():
        return pltpu.make_async_copy(GS.at[y], GM.at[y], own_sem.at[2])

    def own_gz():
        return pltpu.make_async_copy(GO.at[z], GR.at[z], own_sem.at[3])

    def gate_start():
        row = iota((COLUMN, BLOCK), 0)
        spread = row - SLOTS * jnp.floor((row + 0.5) * (1.0 / SLOTS)) == iota((COLUMN, BLOCK), 1)
        lane = iota((NZ, COLUMN), 1)
        gather = one_where(jnp.floor((lane + 0.5) * (1.0 / SLOTS)) == iota((NZ, COLUMN), 0))
        for yy in range(NY):
            column = jnp.sum(gacc[yy], axis=1, keepdims=True)
            value = jnp.where(spread, column, 0.0)
            total = jnp.zeros((NZ, BLOCK), F32)
            for _ in range(3):
                digit = value.astype(BF)
                total = total + jnp.dot(gather, digit, preferred_element_type=F32)
                value = value - digit.astype(F32)
            GS[yy] = total
        for d in range(1, NY):
            remote(GS.at[lax.rem(y + d, NY)], GM.at[y], gy_sem.at[0], gy_sem.at[1], ypeer(d)).start()
        own_gy().start()

    def gate_mid():
        three = GM.at[pl.ds(0, NY - 1)]
        remote(three, three, gy_sem.at[0], gy_sem.at[1], ypeer(1)).wait_recv()
        own_gy().wait()
        for yy in range(NY):
            for zz in range(NZ):
                GO[zz, yy : yy + 1, :] = GM[yy, zz : zz + 1, :]
        for d in range(1, NZ):
            remote(GO.at[zat(d)], GR.at[z], gz_sem.at[0], gz_sem.at[1], zpeer(d)).start()
        own_gz().start()

    def gate_end():
        most = GR.at[pl.ds(0, NZ - 1)]
        remote(most, most, gz_sem.at[0], gz_sem.at[1], zpeer(1)).wait_recv()
        own_gz().wait()
        for zz in range(NZ):
            G2[zz * NY : (zz + 1) * NY, :] = GR[zz, 0:NY, :]
        table = G2[...]
        ranks = RK[...]
        value = jnp.zeros((EXPERTS, TOK), F32)
        for s in range(SLOTS):
            value = value + jnp.where(ranks == float(s), table[:, s : s + 1], 0.0)
        for k in range(TOP):
            named = routes[k : k + 1, :].astype(F32)
            gate_o[k : k + 1, :] = jnp.sum(
                jnp.where(iota((EXPERTS, TOK), 0) == named, value, 0.0), axis=0, keepdims=True
            )

    def ring_half(m, h):
        for a in (3, 2, 1, 0):
            s = 2 * a + h
            if s == 0:

                @pl.when(m + 2 < ND)
                def _():
                    for way in range(2):
                        ring_copy(way, m + 2, 0).start()

            else:

                @pl.when(jnp.logical_and(m >= a, m - a < ND))
                def _(s=s, a=a):
                    for way in range(2):
                        if s < steps[way]:
                            ring_arrival(way, m - a, s - 1)
                            ring_copy(way, m - a, s).start()

    def body(m, carry):
        ring_half(m, 0)

        @pl.when(jnp.logical_and(m >= 4, m < ND + 4))
        def _():
            select(m - 4)

        @pl.when(m == 4)
        def _():
            hidden_end()

        ring_half(m, 1)

        @pl.when(jnp.logical_and(m >= 5, m < ND + 5))
        def _():
            products(m - 5)

        @pl.when(m == 3)
        def _():
            hidden_mid()

        @pl.when(m == ND + 4)
        def _():
            gate_start()

        @pl.when(m == ND + 5)
        def _():
            gate_mid()

        @pl.when(m >= 6)
        def _():
            finish(m - 6)

        return carry

    lax.fori_loop(0, ND + 6, body, 0)
    gate_end()

    def drain(c, carry):
        for way in range(2):
            sent = G.at[c, pl.ds(0, steps[way])]
            remote(sent, sent, ring_send.at[way, c], ring_recv.at[way, c, 0], zpeer(1)).wait_send()
        three = YS.at[c, pl.ds(0, NY - 1)]
        remote(three, three, ys_send.at[c], ys_recv.at[c], ypeer(1)).wait_send()
        seven = XS.at[c, pl.ds(0, NR - 1)]
        remote(seven, seven, xs_send.at[c], xs_recv.at[c], xpeer(1)).wait_send()
        return carry

    lax.fori_loop(0, ND, drain, 0)
    most = PK.at[pl.ds(0, NZ - 1)]
    remote(most, most, hz_sem.at[0], hz_sem.at[1], zpeer(1)).wait_send()
    three = YH.at[pl.ds(0, NY - 1)]
    remote(three, three, hy_sem.at[0], hy_sem.at[1], ypeer(1)).wait_send()
    three = GS.at[pl.ds(0, NY - 1)]
    remote(three, three, gy_sem.at[0], gy_sem.at[1], ypeer(1)).wait_send()
    most = GO.at[pl.ds(0, NZ - 1)]
    remote(most, most, gz_sem.at[0], gz_sem.at[1], zpeer(1)).wait_send()


def per_device(cotangent, hidden, routes, numerators, w_down):
    whole = pl.BlockSpec(memory_space=pl.ANY)
    vmem = pl.BlockSpec(memory_space=pltpu.VMEM)
    dma = pltpu.SemaphoreType.DMA
    gate, scales, grad = pl.pallas_call(
        kernel,
        out_shape=(
            jax.ShapeDtypeStruct((TOP, TOK), F32),
            jax.ShapeDtypeStruct((SHARE, BLOCK), F32),
            jax.ShapeDtypeStruct((SHARE, WIDTH), F32),
        ),
        in_specs=[whole, whole, vmem, vmem, whole],
        out_specs=(vmem, vmem, vmem),
        scratch_shapes=[
            pltpu.VMEM((ND, NZ, TOK, DC), BF),
            pltpu.VMEM((NZ, PLANE, PADH), BF),
            pltpu.VMEM((NZ, PLANE, PADH), BF),
            pltpu.VMEM((NY, COLUMN, PADH), BF),
            pltpu.VMEM((NY * COLUMN, PADH), BF),
            pltpu.VMEM((PADH, ROUTED), BF),
            pltpu.VMEM((PADH, NY * COLUMN), BF),
            pltpu.VMEM((ND, PADH, DC), BF),
            pltpu.VMEM((2, NY * GROUP, HALF * TOK), BF),
            pltpu.VMEM((ND, NY, COLUMN, DC), BF),
            pltpu.VMEM((ND, NY, COLUMN, DC), BF),
            pltpu.VMEM((ND, NR, SHARE, DC), BF),
            pltpu.VMEM((ND, NR, SHARE, DC), BF),
            pltpu.VMEM((NY, COLUMN, BLOCK), F32),
            pltpu.VMEM((EXPERTS, TOK), F32),
            pltpu.VMEM((NY, NZ, BLOCK), F32),
            pltpu.VMEM((NY, NZ, BLOCK), F32),
            pltpu.VMEM((NZ, 8, BLOCK), F32),
            pltpu.VMEM((NZ, 8, BLOCK), F32),
            pltpu.VMEM((EXPERTS, BLOCK), F32),
            dma((ND,)),
            dma((TOP,)),
            dma((ND,)),
            dma((4,)),
            dma((ND,)),
            dma((ND,)),
            dma((2, ND)),
            dma((2, ND, HALF)),
            dma((2,)),
            dma((2,)),
            dma((ND,)),
            dma((ND,)),
            dma((ND,)),
            dma((ND,)),
            dma((2,)),
            dma((2,)),
        ],
        compiler_params=pltpu.CompilerParams(
            collective_id=0, has_side_effects=True, vmem_limit_bytes=60 * 1024 * 1024
        ),
    )(
        cotangent,
        hidden.transpose(1, 2, 0),
        routes.T,
        numerators.T,
        w_down[0],
    )
    return gate.T, scales[None, :, : WIDTH // BLOCK], grad[None]


def solution(mesh):
    return jax.shard_map(
        per_device,
        mesh=mesh,
        in_specs=(
            P(("expert", "replica"), None),
            P(("expert", "replica"), None, None),
            P(("expert", "replica"), None),
            P(("expert", "replica"), None),
            P("expert", None, None),
        ),
        out_specs=(
            P(("expert", "replica"), None),
            P("expert", "replica", None),
            P("expert", "replica", None),
        ),
        check_vma=False,
    )
```

time: 617 us -> 236 us (0.38)
  waiting for transfers between devices: 409 us -> 0 us
  Pallas kernels: 0 us -> 230 us
  local copies, waits for them, and re-layouts: 79.6 us -> 4.75 us
  starting transfers between devices: 52.3 us -> 0 us
  blocking collectives: 28.4 us -> 0 us
  other arithmetic: 15.9 us -> 0 us
  matrix products: 15.8 us -> 0 us
  between operations: 14.2 us -> 0.64 us
    all_to_all x4 -> x0, waiting for transfers between devices: 371 us -> none  [the longest x1 268 us: per_device(): lax.all_to_all(send_cot, 'expert', split_axis=0, concat_axis=0, tiled=True)]
    pallas_call x0 -> x1, Pallas kernels: none -> 230 us  [per_device(): pl.pallas_call(kernel, out_shape=(jax.ShapeDtypeStruct((TOP, TOK), F32),...]
    all_to_all x4 -> x0, starting transfers between devices: 52.1 us -> none  [the longest x1 19.3 us: per_device(): lax.all_to_all(send_w.astype(jnp.bfloat16), 'expert', split_axis=0, conca...]
    psum x1 -> x0, waiting for transfers between devices: 37.2 us -> none  [per_device(): lax.psum(mantissa.astype(jnp.bfloat16), 'replica').astype(jnp.float32)]
    reshape x8 -> x0, local copies, waits for them, and re-layouts: 30.8 us -> none  [the longest x2 7.96 us: per_device(): hid_flat = got_hid.reshape(total_slots, hidden_width)]
    pmax x1 -> x0, blocking collectives: 28.4 us -> none  [per_device(): lax.pmax(local_max.astype(jnp.bfloat16), 'replica').astype(local_max.dtype)]
    gather x4 -> x0, local copies, waits for them, and re-layouts: 24.9 us -> none  [the longest x1 7.27 us: per_device(): send_w = padded_w[source_row].reshape(experts, slot_count)]
    dot_general x2 -> x0, matrix products: 15.8 us -> none  [the longest x1 9.03 us: per_device(): lax.dot_general(hid_flat, scaled, (((0,), (0,)), ((), ())), preferred_ele...]
  transfers between devices with their start and end apart: 5 -> 0, of which waited for: 4 -> 0; matrix products, arithmetic and copies ran while one was open for 9% -> 0% of each run, Pallas kernels for 0% -> 0%
where the time goes in v2:
time: 236 us; the launch traced here: 235 us
  Pallas kernels  230 us (97%)
  local copies, waits for them, and re-layouts  4.75 us (2%)
    pallas_call x1, Pallas kernels, per_device(): pl.pallas_call(kernel, out_shape=(jax.ShapeDtypeStruct((TOP, TOK), F32),...  230 us

profile of v2, /device:TPU:1, one launch (start us, length us, event | category | flops | bytes accessed | tf_op | source)
XLA Modules:
  0.0 235.0 jit_solution(8131509227464031068)
XLA Ops:
  0.6 229.6 %shard_map.76 = (f32[6,128]{1,0:T(8,128)}, f32[88,128]{1,0:T(8,128)}, f32[88,2048]{1,0:T(8,128)}) custom-call(bf16[128,2048]{1,0:T(8,128)(2,1)} %cot.1, bf16[6,704,128]{2,1,0:T(8,128)(2,1)} %bitcast.9, s32[6,128]{1,0:T(8,128)} %bitcast.12, s32[6,128]{1,0:T(8,128)} %bitcast.13, bf16[704,2048]{1,0:T(8,128)(2,1)} %bitcast.8), custom_call_target="tpu_custom_call" | custom-call | tf_op jit(solution)/shard_map/pallas_call | solution.py:417
  230.3 0.8 slice_bitcast_fusion
  231.0 0.7 copy.8
  231.7 1.3 copy.11
  233.0 2.0 copy.12

commit v3 on v2

--- a/solution.py
+++ b/solution.py
@@ -21,6 +21,9 @@
 HALF = NZ // 2
 GROUP = HALF * SLOTS
 PLANE = NY * SLOTS
+STAGGER = 2
+FULL = -(-HALF // STAGGER)
+TURN = 1
 
 
 def iota(shape, dim):
@@ -34,7 +37,7 @@
 def kernel(
     cot, hid6, routes, nums, w,
     gate_o, scale_o, grad_o,
-    G, PK, HZ, YH, HY, hidL, hT, WS, SEL, YS, R, XS, XR, gacc, RK, GS, GM, GO, GR, G2,
+    G, PK, HZ, YH, HY, hidL, hT, WS, SEL, YS, R, XS, XR, gacc, RK, GS, GM, GO, GR, G2, VS, scales,
     cot_sem, hid_sem, w_sem, own_sem, ylocal, xlocal,
     ring_send, ring_recv, hz_sem, hy_sem, ys_send, ys_recv, xs_send, xs_recv, gy_sem, gz_sem,
 ):
@@ -90,8 +93,6 @@
         pl.semaphore_signal(barrier, inc=1, device_id=peer, device_id_type=MESH)
     pl.semaphore_wait(barrier, len(peers))
 
-    steps = (HALF - 1, HALF)
-
     def ring_copy(way, j, s):
         slot = zat(NZ - s) if way == 0 else zat(s)
         peer = zpeer(1) if way == 0 else zpeer(NZ - 1)
@@ -104,9 +105,8 @@
         here = G.at[j, slot]
         remote(here, here, ring_send.at[way, j], ring_recv.at[way, j, s], peer).wait_recv()
 
-    for copy in cot_loads:
-        copy.wait()
-    for j in range(2):
+    for j in range(ND):
+        cot_loads[j].wait()
         for way in range(2):
             ring_copy(way, j, 0).start()
 
@@ -206,6 +206,28 @@
 
         lax.fori_loop(0, NY * COLUMN // TOK, turn, 0)
 
+    def drain_ring(c, carry):
+        for way in range(2):
+            sent = G.at[c, pl.ds(0, HALF - 1)]
+            remote(sent, sent, ring_send.at[way, c], ring_recv.at[way, c, 0], zpeer(1)).wait_send()
+
+            @pl.when(lax.rem(c + way, 2) == 1)
+            def _(way=way):
+                more = G.at[c, 0]
+                remote(more, more, ring_send.at[way, c], ring_recv.at[way, c, 0], zpeer(1)).wait_send()
+
+        return carry
+
+    def drain_rows(c, carry):
+        three = YS.at[c, pl.ds(0, NY - 1)]
+        remote(three, three, ys_send.at[c], ys_recv.at[c], ypeer(1)).wait_send()
+        return carry
+
+    def drain_parts(c, carry):
+        seven = XS.at[c, pl.ds(0, NR - 1)]
+        remote(seven, seven, xs_send.at[c], xs_recv.at[c], xpeer(1)).wait_send()
+        return carry
+
     def own_y(c):
         return pltpu.make_async_copy(YS.at[c, y], R.at[c, y], ylocal.at[c])
 
@@ -214,7 +236,12 @@
 
     def select(c):
         for way in range(2):
-            ring_arrival(way, c, steps[way] - 1)
+
+            @pl.when(lax.rem(c + way, 2) == 1)
+            def _(way=way):
+                ring_arrival(way, c, HALF - 1)
+                ring_arrival(1 - way, c, HALF - 2)
+
         for g in range(2):
             block = G[c, g * HALF : (g + 1) * HALF].reshape(HALF * TOK, DC)
             out = jnp.dot(SEL[g], block, preferred_element_type=F32).astype(BF)
@@ -227,9 +254,39 @@
         own_y(c).start()
 
     def products(c):
+        def ahead(b, carry):
+            rows = HY[pl.ds(pl.multiple_of(b * COLUMN, COLUMN), COLUMN), :]
+            VS[b] = jnp.dot(rows, WS[c], preferred_element_type=F32)
+            return carry
+
+        lax.fori_loop(0, NY, ahead, 0)
+
+        @pl.when(c == ND - 1)
+        def _():
+            lax.fori_loop(0, ND, drain_ring, 0)
+            lax.fori_loop(0, ND - 1, drain_rows, 0)
+            most = PK.at[pl.ds(0, NZ - 1)]
+            remote(most, most, hz_sem.at[0], hz_sem.at[1], zpeer(1)).wait_send()
+            half = YH.at[pl.ds(0, NY - 1)]
+            remote(half, half, hy_sem.at[0], hy_sem.at[1], ypeer(1)).wait_send()
+
         three = R.at[c, pl.ds(0, NY - 1)]
         remote(three, three, ys_send.at[c], ys_recv.at[c], ypeer(1)).wait_recv()
         own_y(c).wait()
+
+        def gates(b, carry):
+            value = VS[b] * R[c, b].astype(F32)
+            total = value[:, :BLOCK]
+            for p in range(1, DC // BLOCK):
+                total = total + value[:, p * BLOCK : (p + 1) * BLOCK]
+            gacc[b] = gacc[b] + total
+            return carry
+
+        lax.fori_loop(0, NY, gates, 0)
+
+        @pl.when(c == ND - 1)
+        def _():
+            gate_start()
 
         def part(i, carry):
             start = pl.multiple_of(i * (HID // 2), HID // 2)
@@ -247,17 +304,6 @@
                 XS.at[c, lax.rem(rep + d, NR)], XR.at[c, rep], xs_send.at[c], xs_recv.at[c], xpeer(d)
             ).start()
         own_x(c).start()
-
-        def gates(b, carry):
-            rows = HY[pl.ds(pl.multiple_of(b * COLUMN, COLUMN), COLUMN), :]
-            value = jnp.dot(rows, WS[c], preferred_element_type=F32) * R[c, b].astype(F32)
-            total = value[:, :BLOCK]
-            for p in range(1, DC // BLOCK):
-                total = total + value[:, p * BLOCK : (p + 1) * BLOCK]
-            gacc[b] = gacc[b] + total
-            return carry
-
-        lax.fori_loop(0, NY, gates, 0)
 
     def finish(c):
         seven = XR.at[c, pl.ds(0, NR - 1)]
@@ -269,16 +315,15 @@
             value = XR[c, q].astype(F32)
             total = total + value
             largest = jnp.maximum(largest, jnp.abs(value))
-        lane = iota((SHARE, BLOCK), 1)
         for p in range(DC // BLOCK):
             cols = slice(p * BLOCK, (p + 1) * BLOCK)
             scale = jnp.max(largest[:, cols], axis=1, keepdims=True) + 1e-6
             start = pl.multiple_of(c * DC + p * BLOCK, BLOCK)
             grad_o[:, pl.ds(start, BLOCK)] = total[:, cols] / scale
             number = (c * (DC // BLOCK) + p).astype(F32)
-            scale_o[...] = jnp.where(lane == number, scale, scale_o[...])
-
-    scale_o[...] = jnp.zeros_like(scale_o)
+            scales[...] = jnp.where(iota((SHARE, BLOCK), 1) == number, scale, scales[...])
+
+    scales[...] = jnp.zeros_like(scales)
 
     def own_gy():
         return pltpu.make_async_copy(GS.at[y], GM.at[y], own_sem.at[2])
@@ -332,78 +377,70 @@
                 jnp.where(iota((EXPERTS, TOK), 0) == named, value, 0.0), axis=0, keepdims=True
             )
 
-    def ring_half(m, h):
-        for a in (3, 2, 1, 0):
-            s = 2 * a + h
-            if s == 0:
-
-                @pl.when(m + 2 < ND)
-                def _():
+    last = HALF - 1
+
+    def ring_steps(m, h):
+        for s in range(last, 0, -1):
+            if s % STAGGER != h:
+                continue
+            j = m - s // STAGGER
+            valid = jnp.logical_and(j >= 0, j < ND)
+
+            if s < last:
+
+                @pl.when(valid)
+                def _(s=s, j=j):
                     for way in range(2):
-                        ring_copy(way, m + 2, 0).start()
+                        ring_arrival(way, j, s - 1)
+                        ring_copy(way, j, s).start()
 
             else:
-
-                @pl.when(jnp.logical_and(m >= a, m - a < ND))
-                def _(s=s, a=a):
-                    for way in range(2):
-                        if s < steps[way]:
-                            ring_arrival(way, m - a, s - 1)
-                            ring_copy(way, m - a, s).start()
+                for way in range(2):
+
+                    @pl.when(jnp.logical_and(valid, lax.rem(j + way, 2) == 1))
+                    def _(s=s, j=j, way=way):
+                        ring_arrival(way, j, s - 1)
+                        ring_copy(way, j, s).start()
 
     def body(m, carry):
-        ring_half(m, 0)
-
-        @pl.when(jnp.logical_and(m >= 4, m < ND + 4))
-        def _():
-            select(m - 4)
-
-        @pl.when(m == 4)
+        ring_steps(m, 0)
+
+        @pl.when(jnp.logical_and(m >= FULL, m < ND + FULL))
+        def _():
+            select(m - FULL)
+
+        @pl.when(m == FULL)
         def _():
             hidden_end()
 
-        ring_half(m, 1)
-
-        @pl.when(jnp.logical_and(m >= 5, m < ND + 5))
-        def _():
-            products(m - 5)
-
-        @pl.when(m == 3)
+        for h in range(1, STAGGER):
+            ring_steps(m, h)
+
+        @pl.when(jnp.logical_and(m >= FULL + 1, m < ND + FULL + 1))
+        def _():
+            products(m - FULL - 1)
+
+        @pl.when(m == TURN)
         def _():
             hidden_mid()
 
-        @pl.when(m == ND + 4)
-        def _():
-            gate_start()
-
-        @pl.when(m == ND + 5)
+        @pl.when(m == ND + FULL + 1)
         def _():
             gate_mid()
-
-        @pl.when(m >= 6)
-        def _():
-            finish(m - 6)
+            lax.fori_loop(0, ND - 1, drain_parts, 0)
+
+        @pl.when(m >= FULL + 2)
+        def _():
+            finish(m - FULL - 2)
 
         return carry
 
-    lax.fori_loop(0, ND + 6, body, 0)
+    lax.fori_loop(0, ND + FULL + 2, body, 0)
     gate_end()
 
-    def drain(c, carry):
-        for way in range(2):
-            sent = G.at[c, pl.ds(0, steps[way])]
-            remote(sent, sent, ring_send.at[way, c], ring_recv.at[way, c, 0], zpeer(1)).wait_send()
-        three = YS.at[c, pl.ds(0, NY - 1)]
-        remote(three, three, ys_send.at[c], ys_recv.at[c], ypeer(1)).wait_send()
-        seven = XS.at[c, pl.ds(0, NR - 1)]
-        remote(seven, seven, xs_send.at[c], xs_recv.at[c], xpeer(1)).wait_send()
-        return carry
-
-    lax.fori_loop(0, ND, drain, 0)
-    most = PK.at[pl.ds(0, NZ - 1)]
-    remote(most, most, hz_sem.at[0], hz_sem.at[1], zpeer(1)).wait_send()
-    three = YH.at[pl.ds(0, NY - 1)]
-    remote(three, three, hy_sem.at[0], hy_sem.at[1], ypeer(1)).wait_send()
+    scale_o[...] = jnp.transpose(scales[...])[: WIDTH // BLOCK, :]
+    lax.fori_loop(ND - 1, ND, drain_rows, 0)
+    lax.fori_loop(ND - 1, ND, drain_parts, 0)
     three = GS.at[pl.ds(0, NY - 1)]
     remote(three, three, gy_sem.at[0], gy_sem.at[1], ypeer(1)).wait_send()
     most = GO.at[pl.ds(0, NZ - 1)]
@@ -418,7 +455,7 @@
         kernel,
         out_shape=(
             jax.ShapeDtypeStruct((TOP, TOK), F32),
-            jax.ShapeDtypeStruct((SHARE, BLOCK), F32),
+            jax.ShapeDtypeStruct((WIDTH // BLOCK, SHARE), F32),
             jax.ShapeDtypeStruct((SHARE, WIDTH), F32),
         ),
         in_specs=[whole, whole, vmem, vmem, whole],
@@ -444,6 +481,8 @@
             pltpu.VMEM((NZ, 8, BLOCK), F32),
             pltpu.VMEM((NZ, 8, BLOCK), F32),
             pltpu.VMEM((EXPERTS, BLOCK), F32),
+            pltpu.VMEM((NY, COLUMN, DC), F32),
+            pltpu.VMEM((SHARE, BLOCK), F32),
             dma((ND,)),
             dma((TOP,)),
             dma((ND,)),
@@ -471,7 +510,7 @@
         numerators.T,
         w_down[0],
     )
-    return gate.T, scales[None, :, : WIDTH // BLOCK], grad[None]
+    return gate.T, scales.T[None], grad[None]
 
 
 def solution(mesh):

time: 236 us -> 225 us (0.953)
  Pallas kernels: 230 us -> 219 us
    pallas_call x1, Pallas kernels: 230 us -> 219 us  [per_device(): pl.pallas_call(kernel, out_shape=(jax.ShapeDtypeStruct((TOP, TOK), F32),...]
where the time goes in v3:
time: 225 us
  Pallas kernels  219 us (97%)
  local copies, waits for them, and re-layouts  4.57 us (2%)
    pallas_call x1, Pallas kernels, per_device(): pl.pallas_call(kernel, out_shape=(jax.ShapeDtypeStruct((TOP, TOK), F32),...  219 us
    unnamed x3, local copies, waits for them, and re-layouts  4.57 us

profile of v3, /device:TPU:1, one launch (start us, length us, event | category | flops | bytes accessed | tf_op | source)
XLA Modules:
  0.0 224.6 jit_solution(17377585794750412090)
XLA Ops:
  0.6 219.4 %shard_map.76 = (f32[6,128]{1,0:T(8,128)}, f32[16,88]{1,0:T(8,128)}, f32[88,2048]{1,0:T(8,128)}) custom-call(bf16[128,2048]{1,0:T(8,128)(2,1)} %cot.1, bf16[6,704,128]{2,1,0:T(8,128)(2,1)} %bitcast.10, s32[6,128]{1,0:T(8,128)} %bitcast.14, s32[6,128]{1,0:T(8,128)} %bitcast.15, bf16[704,2048]{1,0:T(8,128)(2,1)} %bitcast.9), custom_call_target="tpu_custom_call" | custom-call | tf_op jit(solution)/shard_map/pallas_call | solution.py:454
  220.1 1.3 copy.11
  221.3 1.3 copy.12
  222.6 2.0 copy.13

commit v4 on v3

--- a/solution.py
+++ b/solution.py
@@ -13,6 +13,9 @@
 SLOTS = 18
 TOK, WIDTH, HID, TOP = 128, 2048, 704, 6
 PADH = 768
+MAIN = 640
+LOW = 40
+CODES = 3
 ROUTED = TOK * TOP
 COLUMN = NZ * SLOTS
 SHARE = HID // NR
@@ -35,11 +38,11 @@
 
 
 def kernel(
-    cot, hid6, routes, nums, w,
+    cot, hid6, routes_in, nums_in, w,
     gate_o, scale_o, grad_o,
-    G, PK, HZ, YH, HY, hidL, hT, WS, SEL, YS, R, XS, XR, gacc, RK, GS, GM, GO, GR, G2, VS, scales,
+    G, PK, HZ, YH, HY, hidL, hT, WS, SEL, YS, R, XS, XR, gacc, RK, GS, GM, GO, GR, G2, VS, scales, PT, TZ, ENDS, routes, nums,
     cot_sem, hid_sem, w_sem, own_sem, ylocal, xlocal,
-    ring_send, ring_recv, hz_sem, hy_sem, ys_send, ys_recv, xs_send, xs_recv, gy_sem, gz_sem,
+    ring_send, ring_recv, hz_sem, hy_sem, ys_send, ys_recv, xs_send, xs_recv, gy_sem, gz_sem, ht_sem,
 ):
     expert = lax.axis_index("expert")
     rep = lax.axis_index("replica")
@@ -80,7 +83,11 @@
         )
         for j in range(ND)
     ]
-    for copy in cot_loads + hid_loads + w_loads:
+    small_loads = [
+        pltpu.make_async_copy(routes_in, routes, own_sem.at[5]),
+        pltpu.make_async_copy(nums_in, nums, own_sem.at[6]),
+    ]
+    for copy in small_loads + cot_loads + hid_loads + w_loads:
         copy.start()
 
     barrier = pltpu.get_barrier_semaphore()
@@ -110,6 +117,8 @@
         for way in range(2):
             ring_copy(way, j, 0).start()
 
+    for copy in small_loads:
+        copy.wait()
     which = iota((EXPERTS, TOK), 0)
     names = [routes[k : k + 1, :].astype(F32) for k in range(TOP)]
     member = jnp.zeros((EXPERTS, TOK), F32)
@@ -149,14 +158,34 @@
         out = lax.dot_general(
             chosen, hidL[...], (((1,), (1,)), ((), ())), preferred_element_type=F32
         )
-        PK[pl.ds(i * NY, NY)] = out.reshape(NY, PLANE, PADH).astype(BF)
+        PK[pl.ds(i * NY, NY)] = out[:, :MAIN].reshape(NY, PLANE, MAIN).astype(BF)
+        ends = out[:, MAIN:].reshape(NY, PLANE, BLOCK)
+        lane = iota((NY, 8, BLOCK), 2)
+        codes = jnp.zeros((NY, 8, BLOCK), F32)
+        for q in range(PLANE // 8):
+            first = BLOCK // 2 + CODES * q
+            moved = pltpu.roll(ends[:, 8 * q : 8 * q + 8, :], CODES * q, 2)
+            here = jnp.logical_and(lane >= first, lane < first + CODES)
+            codes = codes + jnp.where(here, moved, 0.0)
+        for q in range(LOW // 8):
+            low = ends[:, 8 * q : 8 * q + 8, :]
+            if 8 * q + LOW < PLANE:
+                start = 8 * q + LOW
+                high = pltpu.roll(ends[:, start : start + 8, :], BLOCK // 2, 2)
+            else:
+                high = codes
+            line = jnp.where(lane < BLOCK // 2, low, high)
+            PT[pl.ds(i * NY, NY), 8 * q : 8 * q + 8, :] = line.astype(BF)
         return carry
 
     lax.fori_loop(0, NZ // NY, pack, 0)
     for d in (8, 7, 9, 6, 10, 5, 11, 4, 12, 3, 13, 2, 14, 1, 15):
         remote(PK.at[zat(d)], HZ.at[z], hz_sem.at[0], hz_sem.at[1], zpeer(d)).start()
+        remote(PT.at[zat(d)], TZ.at[z], ht_sem.at[0], ht_sem.at[1], zpeer(d)).start()
     own_hz = pltpu.make_async_copy(PK.at[z], HZ.at[z], own_sem.at[0])
     own_hz.start()
+    own_tz = pltpu.make_async_copy(PT.at[z], TZ.at[z], own_sem.at[4])
+    own_tz.start()
     for copy in w_loads:
         copy.wait()
 
@@ -170,6 +199,9 @@
             HZ.at[pl.ds(0, NZ - 1)], HZ.at[pl.ds(0, NZ - 1)], hz_sem.at[0], hz_sem.at[1], zpeer(1)
         ).wait_recv()
         own_hz.wait()
+        most = TZ.at[pl.ds(0, NZ - 1)]
+        remote(most, most, ht_sem.at[0], ht_sem.at[1], zpeer(1)).wait_recv()
+        own_tz.wait()
         out_row = iota((NY * GROUP, 1), 0)
         out_y = jnp.floor((out_row + 0.5) * (1.0 / GROUP))
         rest = out_row - out_y * GROUP
@@ -179,8 +211,25 @@
         permute = one_where(iota((NY * GROUP, NY * GROUP), 1) == source)
         for g in range(2):
             block = HZ[g * HALF : (g + 1) * HALF].astype(F32)
-            block = block.reshape(HALF * PLANE, PADH).astype(BF)
-            out = jnp.dot(permute, block, preferred_element_type=F32)
+            lines = TZ[g * HALF : (g + 1) * HALF].astype(F32)
+            lane = iota((HALF, 8, BLOCK), 2)
+            for q in range(PLANE // 8):
+                start = 8 * q if 8 * q < LOW else 8 * q - LOW
+                values = lines[:, start : start + 8, :]
+                if 8 * q >= LOW:
+                    values = pltpu.roll(values, BLOCK // 2, 2)
+                codes = pltpu.roll(lines[:, LOW - 8 : LOW, :], (BLOCK - CODES * q) % BLOCK, 2)
+                kept = jnp.where(lane < BLOCK // 2 + CODES, codes, 0.0)
+                ENDS[:, 8 * q : 8 * q + 8, :] = jnp.where(lane < BLOCK // 2, values, kept)
+            main = block.reshape(HALF * PLANE, MAIN).astype(BF)
+            ends = ENDS[...].reshape(HALF * PLANE, BLOCK).astype(BF)
+            out = jnp.concatenate(
+                [
+                    jnp.dot(permute, main, preferred_element_type=F32),
+                    jnp.dot(permute, ends, preferred_element_type=F32),
+                ],
+                axis=1,
+            )
             token = out[:, HID + 2 : HID + 3]
             target = jnp.where(token > 0.5, token + out_z * TOK - 1.0, -1.0)
             SEL[g] = one_where(iota((NY * GROUP, HALF * TOK), 1) == target)
@@ -267,6 +316,8 @@
             lax.fori_loop(0, ND - 1, drain_rows, 0)
             most = PK.at[pl.ds(0, NZ - 1)]
             remote(most, most, hz_sem.at[0], hz_sem.at[1], zpeer(1)).wait_send()
+            most = PT.at[pl.ds(0, NZ - 1)]
+            remote(most, most, ht_sem.at[0], ht_sem.at[1], zpeer(1)).wait_send()
             half = YH.at[pl.ds(0, NY - 1)]
             remote(half, half, hy_sem.at[0], hy_sem.at[1], ypeer(1)).wait_send()
 
@@ -448,7 +499,7 @@
 
 
 def per_device(cotangent, hidden, routes, numerators, w_down):
-    whole = pl.BlockSpec(memory_space=pl.ANY)
+    whole = pl.BlockSpec(memory_space=pltpu.HBM)
     vmem = pl.BlockSpec(memory_space=pltpu.VMEM)
     dma = pltpu.SemaphoreType.DMA
     gate, scales, grad = pl.pallas_call(
@@ -458,12 +509,12 @@
             jax.ShapeDtypeStruct((WIDTH // BLOCK, SHARE), F32),
             jax.ShapeDtypeStruct((SHARE, WIDTH), F32),
         ),
-        in_specs=[whole, whole, vmem, vmem, whole],
+        in_specs=[whole] * 5,
         out_specs=(vmem, vmem, vmem),
         scratch_shapes=[
             pltpu.VMEM((ND, NZ, TOK, DC), BF),
-            pltpu.VMEM((NZ, PLANE, PADH), BF),
-            pltpu.VMEM((NZ, PLANE, PADH), BF),
+            pltpu.VMEM((NZ, PLANE, MAIN), BF),
+            pltpu.VMEM((NZ, PLANE, MAIN), BF),
             pltpu.VMEM((NY, COLUMN, PADH), BF),
             pltpu.VMEM((NY * COLUMN, PADH), BF),
             pltpu.VMEM((PADH, ROUTED), BF),
@@ -483,10 +534,15 @@
             pltpu.VMEM((EXPERTS, BLOCK), F32),
             pltpu.VMEM((NY, COLUMN, DC), F32),
             pltpu.VMEM((SHARE, BLOCK), F32),
+            pltpu.VMEM((NZ, LOW, BLOCK), BF),
+            pltpu.VMEM((NZ, LOW, BLOCK), BF),
+            pltpu.VMEM((HALF, PLANE, BLOCK), F32),
+            pltpu.VMEM((TOP, TOK), jnp.int32),
+            pltpu.VMEM((TOP, TOK), jnp.int32),
             dma((ND,)),
             dma((TOP,)),
             dma((ND,)),
-            dma((4,)),
+            dma((7,)),
             dma((ND,)),
             dma((ND,)),
             dma((2, ND)),
@@ -499,9 +555,10 @@
             dma((ND,)),
             dma((2,)),
             dma((2,)),
+            dma((2,)),
         ],
         compiler_params=pltpu.CompilerParams(
-            collective_id=0, has_side_effects=True, vmem_limit_bytes=60 * 1024 * 1024
+            collective_id=0, has_side_effects=True, vmem_limit_bytes=52 * 1024 * 1024
         ),
     )(
         cotangent,

time: 225 us -> 218 us (0.969)
  Pallas kernels: 219 us -> 212 us
    pallas_call x1, Pallas kernels: 219 us -> 212 us  [per_device(): pl.pallas_call(kernel, out_shape=(jax.ShapeDtypeStruct((TOP, TOK), F32),...]
    unnamed x3 -> x9, local copies, waits for them, and re-layouts: 4.57 us -> 4.46 us
where the time goes in v4:
time: 218 us
  Pallas kernels  212 us (97%)
  local copies, waits for them, and re-layouts  4.46 us (2%)
    pallas_call x1, Pallas kernels, per_device(): pl.pallas_call(kernel, out_shape=(jax.ShapeDtypeStruct((TOP, TOK), F32),...  212 us
    unnamed x9, local copies, waits for them, and re-layouts  4.46 us

profile of v4, /device:TPU:1, one launch (start us, length us, event | category | flops | bytes accessed | tf_op | source)
XLA Modules:
  0.0 217.6 jit_solution(4658990313042280287)
XLA Ops:
  0.6 0.0 copy-start
  0.6 1.0 copy-done
  1.7 0.0 copy-start.1
  1.7 0.7 copy-done.1
  2.4 0.0 copy-start.2
  2.4 0.7 copy-done.2
  3.0 212.5 %shard_map.76 = (f32[6,128]{1,0:T(8,128)S(1)}, f32[16,88]{1,0:T(8,128)S(1)}, f32[88,2048]{1,0:T(8,128)S(1)}) custom-call(bf16[128,2048]{1,0:T(8,128)(2,1)S(1)} %copy-done, bf16[6,704,128]{2,1,0:T(8,128)(2,1)} %bitcast.15, s32[6,128]{1,0:T(8,128)S(1)} %bitcast.12, s32[6,128]{1,0:T(8,128)S(1)} %bitcast.13, bf16[704,2048]{1,0:T(8,128)(2,1)} %bitcast.14), custom_call_target="tpu_custom_call" | custom-call | tf_op jit(solution)/shard_map/pallas_call | solution.py:505
  215.5 0.6 copy.11
  216.1 0.6 copy.12
  216.7 0.9 copy.13
Async XLA Ops:
  0.6 1.0 copy-start
  1.7 0.7 copy-start.1
  2.4 0.7 copy-start.2

commit v5 on v4

--- a/solution.py
+++ b/solution.py
@@ -16,6 +16,7 @@
 MAIN = 640
 LOW = 40
 CODES = 3
+HOME = 3
 ROUTED = TOK * TOP
 COLUMN = NZ * SLOTS
 SHARE = HID // NR
@@ -27,6 +28,7 @@
 STAGGER = 2
 FULL = -(-HALF // STAGGER)
 TURN = 1
+NEAR = 2
 
 
 def iota(shape, dim):
@@ -68,7 +70,7 @@
         )
 
     cot_loads = [
-        pltpu.make_async_copy(cot.at[:, pl.ds(j * DC, DC)], G.at[j, z], cot_sem.at[j])
+        pltpu.make_async_copy(cot.at[:, pl.ds(j * DC, DC)], G.at[j, HOME], cot_sem.at[j])
         for j in range(ND)
     ]
     hid_loads = [
@@ -101,16 +103,15 @@
     pl.semaphore_wait(barrier, len(peers))
 
     def ring_copy(way, j, s):
-        slot = zat(NZ - s) if way == 0 else zat(s)
+        step = NZ - 1 if way == 0 else 1
+        held, later = (HOME + step * s) % NZ, (HOME + step * (s + 1)) % NZ
         peer = zpeer(1) if way == 0 else zpeer(NZ - 1)
-        here = G.at[j, slot]
-        return remote(here, here, ring_send.at[way, j], ring_recv.at[way, j, s], peer)
+        return remote(
+            G.at[j, held], G.at[j, later], ring_send.at[way, j], ring_recv.at[way, j, s], peer
+        )
 
     def ring_arrival(way, j, s):
-        slot = zat(NZ - 1 - s) if way == 0 else zat(1 + s)
-        peer = zpeer(1) if way == 0 else zpeer(NZ - 1)
-        here = G.at[j, slot]
-        remote(here, here, ring_send.at[way, j], ring_recv.at[way, j, s], peer).wait_recv()
+        ring_copy(way, j, s).wait_recv()
 
     for j in range(ND):
         cot_loads[j].wait()
@@ -180,11 +181,11 @@
 
     lax.fori_loop(0, NZ // NY, pack, 0)
     for d in (8, 7, 9, 6, 10, 5, 11, 4, 12, 3, 13, 2, 14, 1, 15):
-        remote(PK.at[zat(d)], HZ.at[z], hz_sem.at[0], hz_sem.at[1], zpeer(d)).start()
-        remote(PT.at[zat(d)], TZ.at[z], ht_sem.at[0], ht_sem.at[1], zpeer(d)).start()
-    own_hz = pltpu.make_async_copy(PK.at[z], HZ.at[z], own_sem.at[0])
+        remote(PK.at[zat(d)], HZ.at[(HOME - d) % NZ], hz_sem.at[0], hz_sem.at[1], zpeer(d)).start()
+        remote(PT.at[zat(d)], TZ.at[(HOME - d) % NZ], ht_sem.at[0], ht_sem.at[1], zpeer(d)).start()
+    own_hz = pltpu.make_async_copy(PK.at[z], HZ.at[HOME], own_sem.at[0])
     own_hz.start()
-    own_tz = pltpu.make_async_copy(PT.at[z], TZ.at[z], own_sem.at[4])
+    own_tz = pltpu.make_async_copy(PT.at[z], TZ.at[HOME], own_sem.at[4])
     own_tz.start()
     for copy in w_loads:
         copy.wait()
@@ -283,24 +284,30 @@
     def own_x(c):
         return pltpu.make_async_copy(XS.at[c, rep], XR.at[c, rep], xlocal.at[c])
 
-    def select(c):
-        for way in range(2):
-
-            @pl.when(lax.rem(c + way, 2) == 1)
-            def _(way=way):
-                ring_arrival(way, c, HALF - 1)
-                ring_arrival(1 - way, c, HALF - 2)
-
-        for g in range(2):
-            block = G[c, g * HALF : (g + 1) * HALF].reshape(HALF * TOK, DC)
-            out = jnp.dot(SEL[g], block, preferred_element_type=F32).astype(BF)
-            for yy in range(NY):
-                YS[c, yy, g * GROUP : (g + 1) * GROUP, :] = out[yy * GROUP : (yy + 1) * GROUP]
+    def select(c, g):
+        if g == 1:
+            for way in range(2):
+
+                @pl.when(lax.rem(c + way, 2) == 1)
+                def _(way=way):
+                    ring_arrival(way, c, HALF - 1)
+                    ring_arrival(1 - way, c, HALF - 2)
+
+        block = G[c, g * HALF : (g + 1) * HALF].reshape(HALF * TOK, DC)
+        out = jnp.dot(SEL[g], block, preferred_element_type=F32).astype(BF)
+        rows = pl.ds(g * GROUP, GROUP)
+        for yy in range(NY):
+            YS[c, yy, g * GROUP : (g + 1) * GROUP, :] = out[yy * GROUP : (yy + 1) * GROUP]
         for d in range(1, NY):
             remote(
-                YS.at[c, lax.rem(y + d, NY)], R.at[c, y], ys_send.at[c], ys_recv.at[c], ypeer(d)
+                YS.at[c, lax.rem(y + d, NY), rows],
+                R.at[c, y, rows],
+                ys_send.at[c],
+                ys_recv.at[c],
+                ypeer(d),
             ).start()
-        own_y(c).start()
+        if g == 1:
+            own_y(c).start()
 
     def products(c):
         def ahead(b, carry):
@@ -380,7 +387,7 @@
         return pltpu.make_async_copy(GS.at[y], GM.at[y], own_sem.at[2])
 
     def own_gz():
-        return pltpu.make_async_copy(GO.at[z], GR.at[z], own_sem.at[3])
+        return pltpu.make_async_copy(GO.at[HOME], GR.at[z], own_sem.at[3])
 
     def gate_start():
         row = iota((COLUMN, BLOCK), 0)
@@ -408,7 +415,7 @@
             for zz in range(NZ):
                 GO[zz, yy : yy + 1, :] = GM[yy, zz : zz + 1, :]
         for d in range(1, NZ):
-            remote(GO.at[zat(d)], GR.at[z], gz_sem.at[0], gz_sem.at[1], zpeer(d)).start()
+            remote(GO.at[(d + HOME) % NZ], GR.at[z], gz_sem.at[0], gz_sem.at[1], zpeer(d)).start()
         own_gz().start()
 
     def gate_end():
@@ -458,7 +465,11 @@
 
         @pl.when(jnp.logical_and(m >= FULL, m < ND + FULL))
         def _():
-            select(m - FULL)
+            select(m - FULL, 1)
+
+        @pl.when(jnp.logical_and(m >= NEAR, m < ND + NEAR))
+        def _():
+            select(m - NEAR, 0)
 
         @pl.when(m == FULL)
         def _():
@@ -561,11 +572,16 @@
             collective_id=0, has_side_effects=True, vmem_limit_bytes=52 * 1024 * 1024
         ),
     )(
-        cotangent,
-        hidden.transpose(1, 2, 0),
-        routes.T,
-        numerators.T,
-        w_down[0],
+        *(
+            pltpu.with_memory_space_constraint(value, pltpu.HBM)
+            for value in (
+                cotangent,
+                hidden.transpose(1, 2, 0),
+                routes.T,
+                numerators.T,
+                w_down[0],
+            )
+        )
     )
     return gate.T, scales.T[None], grad[None]
 

time: 218 us -> 216 us (level)
  local copies, waits for them, and re-layouts: 4.46 us -> 2.05 us
    unnamed x9 -> x3, local copies, waits for them, and re-layouts: 4.46 us -> 2.05 us
where the time goes in v5:
time: 216 us
  Pallas kernels  213 us (99%)
    pallas_call x1, Pallas kernels, per_device(): pl.pallas_call(kernel, out_shape=(jax.ShapeDtypeStruct((TOP, TOK), F32),...  213 us

profile of v5, /device:TPU:1, one launch (start us, length us, event | category | flops | bytes accessed | tf_op | source)
XLA Modules:
  0.0 215.6 jit_solution(12576079875819393822)
XLA Ops:
  0.6 212.9 %shard_map.76 = (f32[6,128]{1,0:T(8,128)S(1)}, f32[16,88]{1,0:T(8,128)S(1)}, f32[88,2048]{1,0:T(8,128)S(1)}) custom-call(bf16[128,2048]{1,0:T(8,128)(2,1)} %cot.1, bf16[6,704,128]{2,1,0:T(8,128)(2,1)} %bitcast.13, s32[6,128]{1,0:T(8,128)} %bitcast.14, s32[6,128]{1,0:T(8,128)} %bitcast.15, bf16[704,2048]{1,0:T(8,128)(2,1)} %bitcast.12), custom_call_target="tpu_custom_call" | custom-call | tf_op jit(solution)/shard_map/pallas_call | solution.py:516
  213.6 0.6 copy.11
  214.2 0.6 copy.12
  214.8 0.9 copy.13
